TPU v7x, 512 devices: a whole 4x8x8 slice. The times are simulated.
512 devices in a mesh: pb: 64 (over y_lo, x, z), ka: 8 (over y_hi, core).
Axes of the slice: x: 4, y: 8 (y_hi: 4, y_lo: 2; y = y_hi * 2 + y_lo), z: 8, core: 2. Of those that a mesh axis runs over, the one named last changes fastest.
Arguments:
- queries: bfloat16 [16384, 1024], P('pb'), may hold values from -40 to 40
- keys: bfloat16 [16384, 128], P(('ka', 'pb')), may hold values from -20 to 20
- values: bfloat16 [16384, 128], P(('ka', 'pb')), may hold values from -12 to 12
- dout: bfloat16 [16384, 1024], P('pb'), may hold values from -6 to 6
- block_mask: int32 [128, 128], P('pb', 'ka'), may hold values from 0 to 1, as said below
Outputs:
- attended: bfloat16 [16384, 1024], P('pb', 'ka')
- query_grad: float32 [16384, 1024], P('pb', 'ka')
- key_grad: float32 [16384, 128], P(('ka', 'pb'))
- value_grad: float32 [16384, 128], P(('ka', 'pb'))
Inputs may be any that keep to these rules, and one draw needn't show every extreme that they name: block_mask[i, j] = 1 lets the 128 queries of block i see the 128 keys of block j. Rows 2 * i and 2 * i + 1 are equal; in both of them the entries of columns 2 * i and 2 * i + 1 are 1, and every aligned run of 16 columns holds at least one 1.
All inputs are finite; a program needn't handle non-finite values.
Results may differ from a plain program's by a relative error of at most 0.017.
Values may be sent and summed in bfloat16 or wider, within the bound.
No kernel may reach another device: no remote copies, remote signals or barrier semaphores. Data moves between devices by JAX's collectives and lax.ppermute only.
A program may use at most 64 MiB of HBM per device.

v0:
```python
import math

import jax
import jax.numpy as jnp
from jax import lax
from jax.sharding import PartitionSpec as P

BLOCK = 128


def merged_2(part, axis, combine):
    gathered = jax.tree.map(lambda a: lax.all_gather(a, axis), part)

    def take(source):
        return jax.tree.map(lambda a: lax.dynamic_index_in_dim(a, source, 0, False), gathered)

    return lax.fori_loop(
        1, lax.axis_size(axis), lambda source, state: combine(state, take(source)), take(0)
    )


def tile_live(mask_tile):
    expanded = jnp.repeat(jnp.repeat(mask_tile, BLOCK, axis=0), BLOCK, axis=1)
    return (expanded > 0)[None]


def tile_scores(query_heads, key_tile, score_scale):
    return (
        jnp.einsum("qhd,kd->hqk", query_heads, key_tile, preferred_element_type=jnp.float32)
        * score_scale
    )


def guarded(mask_tile, compute, carry, passive):
    result = lax.cond(jnp.any(mask_tile > 0), compute, passive, carry)
    return result


def fold_parts(part_one, part_two):
    lse_one, out_one = part_one
    lse_two, out_two = part_two
    row_peak = jnp.maximum(lse_one, lse_two)
    joint_lse = row_peak + jnp.log(jnp.exp(lse_one - row_peak) + jnp.exp(lse_two - row_peak))
    mixed_out = (
        out_one * jnp.exp(lse_one - joint_lse)[:, :, None]
        + out_two * jnp.exp(lse_two - joint_lse)[:, :, None]
    )
    return (joint_lse, mixed_out)


def per_device(queries, keys, values, dout, block_mask):
    query_rows, row_width = queries.shape
    head_width = keys.shape[1]
    head_count = row_width // head_width
    heads_own = head_count // lax.axis_size("ka")
    score_scale = 1.0 / math.sqrt(head_width)
    query_heads = queries.reshape(query_rows, head_count, head_width)
    dout_heads = dout.reshape(query_rows, head_count, head_width)
    key_panel, value_panel = (
        lax.all_gather(keys, "pb", axis=0, tiled=True),
        lax.all_gather(values, "pb", axis=0, tiled=True),
    )
    tile_width = BLOCK
    tile_count = key_panel.shape[0] // tile_width
    key_tiles = key_panel.reshape(tile_count, tile_width, head_width)
    value_tiles = value_panel.reshape(tile_count, tile_width, head_width)
    mask_tiles = block_mask.reshape(block_mask.shape[0], tile_count, 1).transpose(1, 0, 2)

    def peak_step(row_max, inputs):
        key_tile, mask_tile = inputs

        def compute(current):
            masked = jnp.where(
                tile_live(mask_tile), tile_scores(query_heads, key_tile, score_scale), -jnp.inf
            )
            return jnp.maximum(current, jnp.max(masked, axis=2))

        return (guarded(mask_tile, compute, row_max, lambda current: current), None)

    max_start = jnp.full((head_count, query_rows), -jnp.inf, jnp.float32)
    panel_max, _ = lax.scan(peak_step, max_start, (key_tiles, mask_tiles))

    def total_step(carry, inputs):
        key_tile, value_tile, mask_tile = inputs

        def compute(running):
            running_total, running_acc = running
            scores = tile_scores(query_heads, key_tile, score_scale)
            weights = jnp.where(tile_live(mask_tile), jnp.exp(scores - panel_max[:, :, None]), 0.0)
            running_acc = running_acc + jnp.einsum(
                "hqk,kd->hqd",
                weights.astype(jnp.bfloat16),
                value_tile,
                preferred_element_type=jnp.float32,
            )
            return (running_total + jnp.sum(weights, axis=2), running_acc)

        return (guarded(mask_tile, compute, carry, lambda running: running), None)

    zeros_total = jnp.zeros((head_count, query_rows), jnp.float32)
    zeros_acc = jnp.zeros((head_count, query_rows, head_width), jnp.float32)
    (panel_total, panel_acc), _ = lax.scan(
        total_step, (zeros_total, zeros_acc), (key_tiles, value_tiles, mask_tiles)
    )
    panel_out = lax.optimization_barrier(
        (panel_acc / panel_total[:, :, None]).astype(jnp.bfloat16)
    ).astype(jnp.float32)
    panel_lse = panel_max + jnp.log(panel_total)
    panel_index = lax.axis_index("ka")
    row_lse, merged = merged_2((panel_lse, panel_out), "ka", fold_parts)
    full_out = merged.astype(jnp.bfloat16)
    row_delta = jnp.sum(
        dout_heads.astype(jnp.float32).transpose(1, 0, 2) * full_out.astype(jnp.float32), axis=2
    )
    own_out = lax.dynamic_slice_in_dim(full_out, panel_index * heads_own, heads_own, 0)
    attended = own_out.transpose(1, 0, 2).reshape(query_rows, heads_own * head_width)

    def grad_step(carry, inputs):
        key_tile, value_tile, mask_tile = inputs

        def compute(grad_acc):
            scores = tile_scores(query_heads, key_tile, score_scale)
            probs = jnp.where(tile_live(mask_tile), jnp.exp(scores - row_lse[:, :, None]), 0.0)
            probs_low = probs.astype(jnp.bfloat16)
            value_part = jnp.einsum(
                "hqk,qhd->kd", probs_low, dout_heads, preferred_element_type=jnp.float32
            )
            dprobs = jnp.einsum(
                "qhd,kd->hqk", dout_heads, value_tile, preferred_element_type=jnp.float32
            )
            dscores = (probs * (dprobs - row_delta[:, :, None])).astype(jnp.bfloat16)
            grad_acc = grad_acc + jnp.einsum(
                "hqk,kd->qhd", dscores, key_tile, preferred_element_type=jnp.float32
            )
            key_part = (
                jnp.einsum("hqk,qhd->kd", dscores, query_heads, preferred_element_type=jnp.float32)
                * score_scale
            )
            return (grad_acc, key_part, value_part)

        def passive(grad_acc):
            blank = jnp.zeros((tile_width, head_width), jnp.float32)
            return (grad_acc, blank, blank)

        grad_acc, key_part, value_part = guarded(mask_tile, compute, carry, passive)
        return (grad_acc, (key_part, value_part))

    grad_start = jnp.zeros((query_rows, head_count, head_width), jnp.float32)
    grad_acc, (key_parts, value_parts) = lax.scan(
        grad_step, grad_start, (key_tiles, value_tiles, mask_tiles)
    )
    panel_dq = lax.optimization_barrier((grad_acc * score_scale).astype(jnp.bfloat16)).astype(
        jnp.float32
    )
    query_grad = lax.psum_scatter(
        panel_dq.reshape(query_rows, row_width).astype(jnp.bfloat16),
        "ka",
        scatter_dimension=1,
        tiled=True,
    ).astype(jnp.float32)
    key_grad, value_grad = (
        lax.psum_scatter(key_parts.reshape(-1, head_width), "pb", scatter_dimension=0, tiled=True),
        lax.psum_scatter(
            value_parts.reshape(-1, head_width), "pb", scatter_dimension=0, tiled=True
        ),
    )
    return (attended, query_grad, key_grad, value_grad)


def solution(mesh):
    in_specs = (
        P("pb", None),
        P(("ka", "pb"), None),
        P(("ka", "pb"), None),
        P("pb", None),
        P("pb", "ka"),
    )
    out_specs = (P("pb", "ka"), P("pb", "ka"), P(("ka", "pb"), None), P(("ka", "pb"), None))
    return jax.shard_map(
        per_device, mesh=mesh, in_specs=in_specs, out_specs=out_specs, check_vma=False
    )
```

profile of v0, /device:TPU:40, one launch (start us, length us, event | category | flops | bytes accessed | tf_op | source)
XLA Modules:
  0.0 1239.2 jit_solution(12552738790059903698)
XLA Ops:
  8.7 164.8 %all_gather.21 = bf16[2048,128]{1,0:T(8,128)(2,1)S(1)} all-gather(bf16[32,128]{1,0:T(8,128)(2,1)} %param.20), channel_id=1, replica_groups=mesh['pb'=64,'ka'=8] {'pb'}, dimensions={0}, use_global_device_ids=true | all-gather | bytes 532480 | tf_op jit(solution)/shard_map/all_gather | solution.py:60
  174.3 22.9 %while.59 = (s32[]{:T(128)}, f32[8,256]{1,0:T(8,128)S(1)}, s32[16,2,1]{1,2,0:T(1,128)S(1)}, bf16[16,128,128]{2,1,0:T(8,128)(2,1)S(1)}, bf16[256,8,128]{2,0,1:T(8,128)(2,1)S(1)}, /*index=5*/s32[]{:T(128)}) while((s32[]{:T(128)}, f32[8,256]{1,0:T(8,128)S(1)}, s32[16,2,1]{1,2,0:T(1,128)S(1)}, bf16[16,128,128]{2,1,0:T(8,128)(2,1)S(1)}, ...), condition=%wide.region_5.6_spmd, body=%wide.region_0.5_spmd.sunk | while | flops 67895304 | bytes 590751 | solution.py:81
  197.2 152.6 %all_gather.22 = bf16[2048,128]{1,0:T(8,128)(2,1)S(1)} all-gather(bf16[32,128]{1,0:T(8,128)(2,1)S(1)} %copy-done), channel_id=1, replica_groups=mesh['pb'=64,'ka'=8] {'pb'}, dimensions={0}, use_global_device_ids=true | all-gather | bytes 532480 | tf_op jit(solution)/shard_map/all_gather | solution.py:61
  349.9 24.8 %while.60 = (s32[]{:T(128)}, f32[8,256]{1,0:T(8,128)S(1)}, f32[8,256,128]{2,1,0:T(8,128)S(1)}, s32[16,2,1]{1,2,0:T(1,128)S(1)}, bf16[16,128,128]{2,1,0:T(8,128)(...) while((s32[]{:T(128)}, f32[8,256]{1,0:T(8,128)S(1)}, ...), condition=%wide.region_11.12_spmd, body=%wide.region_6.11_spmd.sunk | while | flops 135790592 | bytes 3777523 | solution.py:102
  376.3 27.8 %all-gather = f32[64,256]{1,0:T(8,128)S(1)} all-gather(f32[8,256]{1,0:T(8,128)S(1)} %log_add_fusion), channel_id=2, replica_groups=mesh['pb'=64,'ka'=8] {'ka'}, dimensions={0}, use_global_device_ids=true | all-gather | bytes 73728 | tf_op jit(solution)/shard_map/all_gather | solution.py:12
  405.6 64.3 %all-gather.4.cloned.1.call-done = f32[64,256,128]{2,1,0:T(8,128)} async-done(((f32[8,256,128]{2,1,0:T(8,128)}), f32[64,256,128]{2,1,0:T(8,128)}) %all-gather.4.cloned.1.call-update) | async-done | bytes 8388624 | tf_op jit(solution)/shard_map/all_gather | solution.py:12
  469.9 1.3 slice.5
  471.2 15.5 %while.61 = (s32[]{:T(128)}, f32[8,256]{1,0:T(8,128)S(1)}, f32[8,256,128]{2,1,0:T(8,128)S(1)}, f32[8,8,256]{2,1,0:T(8,128)S(1)}, f32[8,8,256,128]{3,2,1,0:T(8,128)}, /*index=5*/s32[]{:T(128)}, s32[]{:T(128)}, s32[]{:T(128)}) while((s32[]{:T(128)}, f32[8,256]{1,0:T(8,128)S(1)}, f32[8,256,128]{2,1,0:T(8,128)S(1)}, ...), condition=%wide.region_13.14_spmd, body=%wide.region_12.13_spmd.sunk | while | flops 800773 | bytes 3219595 | solution.py:17
  471.3 2.1 fusion.61
  473.5 2.1 fusion.61
  475.7 2.1 fusion.61
  477.9 2.1 fusion.61
  480.1 2.1 fusion.61
  482.3 2.1 fusion.61
  484.5 2.1 fusion.61
  487.8 39.1 %while.62 = (s32[]{:T(128)}, f32[256,8,128]{2,0,1:T(8,128)S(1)}, f32[16,128,128]{2,1,0:T(8,128)}, f32[16,128,128]{2,1,0:T(8,128)}, s32[16,2,1]{1,2,0:T(1,128)S(1...) while((s32[]{:T(128)}, f32[256,8,128]{2,0,1:T(8,128)S(1)}, ...), condition=%wide.region_19.20_spmd, body=%wide.region_15.19_spmd.sunk | while | flops 337657856 | bytes 9422343 | solution.py:149
  489.1 1.7 conditional.8
  492.8 1.7 conditional.8
  496.5 1.7 conditional.8
  514.4 1.7 conditional.8
  529.4 1.5 dynamic-slice_bitcast_fusion.2
  530.8 55.8 %reduce-scatter.10.cloned.1.call-done = bf16[128,256]{1,0:T(8,128)(2,1)} async-done(((bf16[1024,256]{1,0:T(8,128)(2,1)}), bf16[128,256]{1,0:T(8,128)(2,1)}) %reduce-scatter.10.cloned.1.call-update) | async-done | bytes 65552
  588.3 325.1 %reduce-scatter.6.cloned.1.call-done = f32[32,128]{1,0:T(8,128)} async-done(((f32[2048,128]{1,0:T(8,128)}), f32[32,128]{1,0:T(8,128)}) %reduce-scatter.6.cloned.1.call-update) | async-done | bytes 16400 | tf_op jit(solution)/shard_map/reduce_scatter | solution.py:162
  913.4 319.3 %reduce-scatter.8.cloned.1.call-done = f32[32,128]{1,0:T(8,128)} async-done(((f32[2048,128]{1,0:T(8,128)}), f32[32,128]{1,0:T(8,128)}) %reduce-scatter.8.cloned.1.call-update) | async-done | bytes 16400 | tf_op jit(solution)/shard_map/reduce_scatter | solution.py:163
  (240 shorter events, 70.4 us)
Async XLA Ops:
  7.2 190.1 %copy-start = (bf16[32,128]{1,0:T(8,128)(2,1)S(1)}, bf16[32,128]{1,0:T(8,128)(2,1)}, u32[]{:S(2)}) copy-start(bf16[32,128]{1,0:T(8,128)(2,1)} %param.21) | copy-start | bytes 24580
  7.2 462.7 %all-gather.4.cloned.1.call-start = ((), (), s32[]{:S(2)}) async-start(), calls=%async_computation.5 | async-start | bytes 9437184 | tf_op jit(solution)/shard_map/all_gather | solution.py:12
  376.2 210.5 %reduce-scatter.10.cloned.1.call-start = ((), (), s32[]{:S(2)}) async-start(), calls=%async_computation.6 | async-start | bytes 589824
  528.0 385.4 %reduce-scatter.6.cloned.1.call-start = ((), (), s32[]{:S(2)}) async-start(), calls=%async_computation.3 | async-start | bytes 1064960 | tf_op jit(solution)/shard_map/reduce_scatter | solution.py:162
  528.8 703.9 %reduce-scatter.8.cloned.1.call-start = ((), (), s32[]{:S(2)}) async-start(), calls=%async_computation.4 | async-start | bytes 1064960 | tf_op jit(solution)/shard_map/reduce_scatter | solution.py:163
Sparse Core Ops, SparseCore 0:
  376.3 93.5 all-gather.3
  528.2 58.4 reduce-scatter.9
  590.1 323.3 reduce-scatter.5
  916.6 316.0 reduce-scatter.7
where the time goes:
time: 1240 us
  waiting for transfers between devices  766 us (62%)
  blocking collectives  345 us (28%)
  other arithmetic  49.2 us (4%)
  loops' own time  33.8 us (3%)
  local copies, waits for them, and re-layouts  20.5 us (2%)
  between operations  13.9 us (1%)
    reduce_scatter x1, waiting for transfers between devices, per_device(): lax.psum_scatter(key_parts.reshape(-1, head_width), 'pb', scatter_dimensi...  325 us
    reduce_scatter x1, waiting for transfers between devices, per_device(): lax.psum_scatter(value_parts.reshape(-1, head_width), 'pb', scatter_dimen...  319 us
    all_gather x1, blocking collectives, per_device(): lax.all_gather(keys, 'pb', axis=0, tiled=True)  165 us
    all_gather x1, blocking collectives, per_device(): lax.all_gather(values, 'pb', axis=0, tiled=True)  153 us
    all_gather x1, waiting for transfers between devices, merged_2(): gathered = jax.tree.map(lambda a: lax.all_gather(a, axis), part)  64.3 us
    unnamed x5, waiting for transfers between devices  57.1 us
    reduce_or x48, other arithmetic, guarded(): result = lax.cond(jnp.any(mask_tile > 0), compute, passive, carry)  30.6 us
    all_gather x1, blocking collectives, merged_2(): gathered = jax.tree.map(lambda a: lax.all_gather(a, axis), part)  27.8 us
  transfers between devices with their start and end apart: 4, of which 4 were waited for; matrix products, arithmetic and copies ran while one was open for 0% of the time, Pallas kernels for 0%

commit v1 on v0

v1 whole, which is shorter than its diff:
```python
import math

import jax
import jax.numpy as jnp
from jax import lax
from jax.experimental import pallas as pl
from jax.experimental.pallas import tpu as pltpu
from jax.sharding import PartitionSpec as P

BLOCK = 128
CHUNK = 256
DEAD = 1.0e30
F32 = jnp.float32
BF16 = jnp.bfloat16


def nt_dot(a, b):
    return lax.dot_general(a, b, (((1,), (1,)), ((), ())), preferred_element_type=F32)


def identity(size):
    rows = lax.broadcasted_iota(jnp.int32, (size, size), 0)
    cols = lax.broadcasted_iota(jnp.int32, (size, size), 1)
    return (rows == cols).astype(F32).astype(BF16)


def forward_kernel(
    mask_ref, kv_ref, q_ref, dout_ref, weights_ref, out_ref, stats_ref, peak_ref, scores, values_t
):
    keys, width = kv_ref.shape[0], kv_ref.shape[1] // 2
    queries, heads = q_ref.shape[0], q_ref.shape[1] // width
    scale = math.log2(math.e) / math.sqrt(width)
    eye = identity(width)
    values_t[...] = nt_dot(eye, kv_ref[:, width:]).astype(BF16)

    def one_head(h, carry):
        cols = pl.ds(pl.multiple_of(h * width, width), width)
        lanes = pl.ds(pl.multiple_of(h * queries, queries), queries)
        query = q_ref[:, cols]
        tops = []
        for start in range(0, keys, CHUNK):
            block = nt_dot(kv_ref[start : start + CHUNK, :width], query) * scale
            scores[start : start + CHUNK, :] = block
            for part in range(0, CHUNK, BLOCK):
                dead = jnp.where(mask_ref[0, (start + part) // BLOCK] > 0, 0.0, DEAD)
                top = jnp.max(block[part : part + BLOCK], axis=0, keepdims=True)
                tops.append((top - dead, dead))
        peak = tops[0][0]
        for top, _ in tops[1:]:
            peak = jnp.maximum(peak, top)
        total = jnp.zeros((1, queries), F32)
        for index, (_, dead) in enumerate(tops):
            start = index * BLOCK
            block = jnp.exp2(scores[start : start + BLOCK, :] - (peak + dead))
            weights_ref[start : start + BLOCK, lanes] = block.astype(BF16)
            total = total + jnp.sum(block, axis=0, keepdims=True)
        acc = jnp.dot(values_t[...], weights_ref[:, lanes], preferred_element_type=F32)
        out = acc / total
        delta = jnp.sum(nt_dot(eye, dout_ref[:, cols]) * out, axis=0, keepdims=True)
        out_ref[h] = out.astype(BF16)
        stats_ref[pl.ds(h, 1), :] = peak + jnp.log2(total)
        stats_ref[pl.ds(heads + h, 1), :] = delta
        peak_ref[pl.ds(h, 1), :] = peak
        return carry

    lax.fori_loop(0, heads, one_head, 0)


def row_mix(stats_ref, heads):
    panels = stats_ref.shape[0]
    top = stats_ref[0, :heads]
    for n in range(1, panels):
        top = jnp.maximum(top, stats_ref[n, :heads])
    total = jnp.zeros_like(top)
    delta = jnp.zeros_like(top)
    for n in range(panels):
        share = jnp.exp2(stats_ref[n, :heads] - top)
        total = total + share
        delta = delta + share * stats_ref[n, heads:]
    return top + jnp.log2(total), delta / total


def backward_kernel(
    stats_ref, peak_ref, kv_ref, q_ref, dout_ref, weights_ref, dq_ref, dkv_ref,
    dscores, keys_t, mixed_q, mixed_dout, factors,
):
    keys, width = kv_ref.shape[0], kv_ref.shape[1] // 2
    queries, heads = q_ref.shape[0], q_ref.shape[1] // width
    scale = 1.0 / math.sqrt(width)
    keys_t[...] = nt_dot(identity(width), kv_ref[:, :width]).astype(BF16)
    row_lse, row_delta = row_mix(stats_ref, heads)
    factor = jnp.exp2(peak_ref[...] - row_lse)
    factors[:heads, :] = factor
    factors[heads:, :] = row_delta
    columns = factor.T
    for h in range(heads):
        rows = slice(h * queries, (h + 1) * queries)
        cols = slice(h * width, (h + 1) * width)
        column = columns[:, h : h + 1]
        mixed_q[rows, :] = (q_ref[:, cols].astype(F32) * column).astype(BF16)
        mixed_dout[rows, :] = (dout_ref[:, cols].astype(F32) * column).astype(BF16)

    def one_head(h, carry):
        cols = pl.ds(pl.multiple_of(h * width, width), width)
        lanes = pl.ds(pl.multiple_of(h * queries, queries), queries)
        cotangent = dout_ref[:, cols]
        delta = factors[pl.ds(heads + h, 1), :]
        for start in range(0, keys, CHUNK):
            rows = slice(start, start + CHUNK)
            dprobs = nt_dot(kv_ref[rows, width:], cotangent)
            dscores[rows, lanes] = (weights_ref[rows, lanes].astype(F32) * (dprobs - delta)).astype(
                BF16
            )
        acc = jnp.dot(keys_t[...], dscores[:, lanes], preferred_element_type=F32)
        dq_ref[h] = (acc * (factors[pl.ds(h, 1), :] * scale)).astype(BF16)
        return carry

    lax.fori_loop(0, heads, one_head, 0)

    def one_chunk(index, carry):
        rows = pl.ds(pl.multiple_of(index * CHUNK, CHUNK), CHUNK)
        key_part = jnp.dot(dscores[rows, :], mixed_q[...], preferred_element_type=F32)
        value_part = jnp.dot(weights_ref[rows, :], mixed_dout[...], preferred_element_type=F32)
        dkv_ref[rows, :width] = (key_part * scale).astype(BF16)
        dkv_ref[rows, width:] = value_part.astype(BF16)
        return carry

    lax.fori_loop(0, keys // CHUNK, one_chunk, 0)


def attended_kernel(own_ref, stats_ref, parts_ref, attended_ref):
    panels, heads = parts_ref.shape[0], stats_ref.shape[1] // 2
    own = own_ref[0]
    row_lse, _ = row_mix(stats_ref, heads)
    picked = lax.broadcasted_iota(jnp.int32, row_lse.shape, 0) == own
    total = jnp.zeros(parts_ref.shape[1:], F32)
    for n in range(panels):
        mixing = jnp.exp2(stats_ref[n, :heads] - row_lse)
        mixing = jnp.sum(jnp.where(picked, mixing, 0.0), axis=0, keepdims=True)
        total = total + parts_ref[n].astype(F32) * mixing
    attended_ref[...] = total.T.astype(BF16)


def finish_kernel(dq_ref, dkv_ref, query_grad_ref, key_grad_ref, value_grad_ref):
    width = key_grad_ref.shape[1]
    total = dq_ref[0].astype(F32)
    for n in range(1, dq_ref.shape[0]):
        total = total + dq_ref[n].astype(F32)
    query_grad_ref[...] = total.T
    both = dkv_ref[0].astype(F32)
    for n in range(1, dkv_ref.shape[0]):
        both = both + dkv_ref[n].astype(F32)
    key_grad_ref[...] = both[:, :width]
    value_grad_ref[...] = both[:, width:]


VMEM = pl.BlockSpec(memory_space=pltpu.VMEM)
SMEM = pl.BlockSpec(memory_space=pltpu.SMEM)


def per_device(queries, keys, values, dout, block_mask):
    rows, row_width = queries.shape
    shard, width = keys.shape
    heads = row_width // width
    pb, ka = lax.axis_size("pb"), lax.axis_size("ka")
    panel = shard * pb
    all_rows = heads * rows
    shape = jax.ShapeDtypeStruct

    both = jnp.concatenate([keys, values], axis=1)
    copies = jnp.broadcast_to(both[None], (pb, shard, 2 * width))
    kv = lax.all_to_all(copies, "pb", 0, 0, tiled=True).reshape(panel, 2 * width)

    weights, out_parts, stats, peak = pl.pallas_call(
        forward_kernel,
        out_shape=(
            shape((panel, all_rows), BF16),
            shape((heads, width, rows), BF16),
            shape((2 * heads, rows), F32),
            shape((heads, rows), F32),
        ),
        in_specs=[SMEM, VMEM, VMEM, VMEM],
        out_specs=(VMEM,) * 4,
        scratch_shapes=[pltpu.VMEM((panel, rows), F32), pltpu.VMEM((width, panel), BF16)],
        name="forward",
    )(block_mask, kv, queries, dout)

    all_stats = lax.all_gather(stats, "ka")
    parts = lax.all_to_all(out_parts, "ka", 0, 0, tiled=True)

    dq_parts, dkv = pl.pallas_call(
        backward_kernel,
        out_shape=(shape((heads, width, rows), BF16), shape((panel, 2 * width), BF16)),
        in_specs=[VMEM] * 6,
        out_specs=(VMEM,) * 2,
        scratch_shapes=[
            pltpu.VMEM((panel, all_rows), BF16),
            pltpu.VMEM((width, panel), BF16),
            pltpu.VMEM((all_rows, width), BF16),
            pltpu.VMEM((all_rows, width), BF16),
            pltpu.VMEM((2 * heads, rows), F32),
        ],
        name="backward",
    )(all_stats, peak, kv, queries, dout, weights)

    own = lax.axis_index("ka").astype(jnp.int32).reshape(1)
    attended = pl.pallas_call(
        attended_kernel,
        out_shape=shape((rows, width), BF16),
        in_specs=[SMEM, VMEM, VMEM],
        out_specs=VMEM,
        name="attended",
    )(own, all_stats, parts)

    dq_own = lax.all_to_all(dq_parts, "ka", 0, 0, tiled=True)
    dkv_own = lax.all_to_all(dkv.reshape(pb, shard, 2 * width), "pb", 0, 0, tiled=True)
    query_grad, key_grad, value_grad = pl.pallas_call(
        finish_kernel,
        out_shape=(shape((rows, width), F32), shape((shard, width), F32), shape((shard, width), F32)),
        in_specs=[VMEM, VMEM],
        out_specs=(VMEM,) * 3,
        name="finish",
    )(dq_own, dkv_own)
    return attended, query_grad, key_grad, value_grad


def solution(mesh):
    in_specs = (
        P("pb", None),
        P(("ka", "pb"), None),
        P(("ka", "pb"), None),
        P("pb", None),
        P("pb", "ka"),
    )
    out_specs = (P("pb", "ka"), P("pb", "ka"), P(("ka", "pb"), None), P(("ka", "pb"), None))
    return jax.shard_map(
        per_device, mesh=mesh, in_specs=in_specs, out_specs=out_specs, check_vma=False
    )
```

time: 1240 us -> 171 us (0.14)
  the two profiles are of different devices: /device:TPU:40 before, /device:TPU:9 now
where the time goes in v1:
time: 171 us
  blocking collectives  88.2 us (52%)
  Pallas kernels  38.1 us (22%)
  waiting for transfers between devices  27.8 us (16%)
  starting transfers between devices  14.1 us (8%)
    all_to_all x1, blocking collectives, per_device(): lax.all_to_all(copies, 'pb', 0, 0, tiled=True).reshape(panel, 2 * width)  44.1 us
    all_to_all x1, waiting for transfers between devices, per_device(): lax.all_to_all(dkv.reshape(pb, shard, 2 * width), 'pb', 0, 0, tiled=True)  27.8 us
    all_gather x1, blocking collectives, per_device(): all_stats = lax.all_gather(stats, 'ka')  24.7 us
    all_to_all x1, blocking collectives, per_device(): dq_own = lax.all_to_all(dq_parts, 'ka', 0, 0, tiled=True)  19.4 us
    pallas_call x1, Pallas kernels, per_device(): pl.pallas_call(backward_kernel, out_shape=(shape((heads, width, rows), BF...  17.4 us
    pallas_call x1, Pallas kernels, per_device(): pl.pallas_call(forward_kernel, out_shape=(shape((panel, all_rows), BF16),...  16.6 us
    all_to_all x1, starting transfers between devices, per_device(): lax.all_to_all(dkv.reshape(pb, shard, 2 * width), 'pb', 0, 0, tiled=True)  7.27 us
    all_to_all x1, starting transfers between devices, per_device(): parts = lax.all_to_all(out_parts, 'ka', 0, 0, tiled=True)  6.83 us
  transfers between devices with their start and end apart: 2, of which 1 were waited for; matrix products, arithmetic and copies ran while one was open for 0% of the time, Pallas kernels for 11%

profile of v1, /device:TPU:9, one launch (start us, length us, event | category | flops | bytes accessed | tf_op | source)
XLA Modules:
  0.0 170.7 jit_solution(16226435109224776268)
XLA Ops:
  0.6 0.7 pad_maximum_fusion
  1.3 0.1 broadcast_in_dim.2
  1.5 44.1 %all_to_all.20 = bf16[64,32,256]{2,1,0:T(8,128)(2,1)} all-to-all(bf16[64,32,256]{2,1,0:T(8,128)(2,1)S(1)} %broadcast_in_dim.2), channel_id=1, replica_groups=mesh['pb'=64,'ka'=8] {'pb'}, dimensions={0} | all-to-all | bytes 2097152 | tf_op jit(solution)/shard_map/all_to_all | solution.py:172
  45.6 16.6 %forward.1 = (bf16[2048,2048]{1,0:T(8,128)(2,1)}, bf16[8,128,256]{2,1,0:T(8,128)(2,1)}, f32[16,256]{1,0:T(8,128)}, f32[8,256]{1,0:T(8,128)}) custom-call(s32[2,16]{1,0:T(2,128)} %mask_ref.1, bf16[2048,256]{1,0:T(8,128)(2,1)} %bitcast.4, bf16[256,1024]{1,0:T(8,128)(2,1)} %q_ref.3, bf16[256,1024]{1,0:T(8,128)(2,1)} %dout_ref.3), custom_call_target="tpu_custom_call" | custom-call | tf_op jit(solution)/shard_map/forward/pallas_call | solution.py:174
  62.1 6.8 %all-to-all-start.1 = ((bf16[8,128,256]{2,1,0:T(8,128)(2,1)}), bf16[8,128,256]{2,1,0:T(8,128)(2,1)S(1)}, u32[]{:S(2)}, u32[]{:S(2)}) async-start(bf16[8,128,256]{2,1,0:T(8,128)(2,1)} %get-tuple-element.14), calls=%async_computation.1 | async-start | bytes 1048576 | tf_op jit(solution)/shard_map/all_to_all | solution.py:189
  68.9 24.7 %all-gather = f32[128,256]{1,0:T(8,128)} all-gather(f32[16,256]{1,0:T(8,128)} %get-tuple-element.13), channel_id=2, replica_groups=mesh['pb'=64,'ka'=8] {'ka'}, dimensions={0}, use_global_device_ids=true | all-gather | bytes 147456 | tf_op jit(solution)/shard_map/all_gather | solution.py:188
  93.7 17.4 %backward.1 = (bf16[8,128,256]{2,1,0:T(8,128)(2,1)}, bf16[2048,256]{1,0:T(8,128)(2,1)}) custom-call(f32[8,16,256]{2,1,0:T(8,128)} %bitcast.6, f32[8,256]{1,0:T(8,128)} %get-tuple-element.15.peak_ref, bf16[2048,256]{1,0:T(8,128)(2,1)} %bitcast.5, bf16[256,1024]{1,0:T(8,128)(2,1)} %q_ref.3, bf16[256,1024]{1,0:T(8,128)(2,1)} %dout_ref.3, ...), custom_call_target="tpu_custom_call" | custom-call | tf_op jit(solution)/shard_map/backward/pallas_call | solution.py:191
  111.1 0.0 all-to-all-done.1.parts_ref
  111.1 0.0 copy-start.1
  111.1 19.4 %all_to_all.21.dq_ref = bf16[8,128,256]{2,1,0:T(8,128)(2,1)} all-to-all(bf16[8,128,256]{2,1,0:T(8,128)(2,1)} %get-tuple-element.17), channel_id=1, replica_groups=mesh['pb'=64,'ka'=8] {'ka'}, dimensions={0} | all-to-all | bytes 1048576 | tf_op jit(solution)/shard_map/all_to_all | solution.py:215
  130.5 7.3 %all-to-all-start.3 = ((bf16[64,32,256]{2,1,0:T(8,128)(2,1)}), bf16[64,32,256]{2,1,0:T(8,128)(2,1)S(1)}, u32[]{:S(2)}, u32[]{:S(2)}) async-start(bf16[64,32,256]{2,1,0:T(8,128)(2,1)} %bitcast.8), calls=%async_computation.3 | async-start | bytes 2097152 | tf_op jit(solution)/shard_map/all_to_all | solution.py:216
  137.8 0.0 copy-done.1
  137.8 2.0 %attended.1 = bf16[256,128]{1,0:T(8,128)(2,1)} custom-call(s32[1]{0:T(128)} %bitcast.own_ref, f32[8,16,256]{2,1,0:T(8,128)} %bitcast.7, bf16[8,128,256]{2,1,0:T(8,128)(2,1)} %copy-done.1), custom_call_target="tpu_custom_call" | custom-call | tf_op jit(solution)/shard_map/attended/pallas_call | solution.py:207
  139.7 27.8 %all-to-all-done.3.dkv_ref = bf16[64,32,256]{2,1,0:T(8,128)(2,1)S(1)} async-done(((bf16[64,32,256]{2,1,0:T(8,128)(2,1)}), bf16[64,32,256]{2,1,0:T(8,128)(2,1)S(1)}, u32[]{:S(2)}, u32[]{:S(2)}) %all-to-all-start.3) | async-done | bytes 1048608 | tf_op jit(solution)/shard_map/all_to_all | solution.py:216
  167.6 0.0 copy-start
  167.6 1.0 copy-done
  168.5 2.2 %finish.1 = (f32[256,128]{1,0:T(8,128)}, f32[32,128]{1,0:T(8,128)}, f32[32,128]{1,0:T(8,128)}) custom-call(bf16[8,128,256]{2,1,0:T(8,128)(2,1)} %all_to_all.21.dq_ref, bf16[64,32,256]{2,1,0:T(8,128)(2,1)} %copy-done), custom_call_target="tpu_custom_call" | custom-call | tf_op jit(solution)/shard_map/finish/pallas_call | solution.py:217
Async XLA Ops:
  62.1 49.0 %all-to-all-start.1 = ((bf16[8,128,256]{2,1,0:T(8,128)(2,1)}), bf16[8,128,256]{2,1,0:T(8,128)(2,1)S(1)}, u32[]{:S(2)}, u32[]{:S(2)}) async-start(bf16[8,128,256]{2,1,0:T(8,128)(2,1)} %get-tuple-element.14), calls=%async_computation.1 | async-start | bytes 1048576 | tf_op jit(solution)/shard_map/all_to_all | solution.py:189
  111.1 26.7 %copy-start.1 = (bf16[8,128,256]{2,1,0:T(8,128)(2,1)}, bf16[8,128,256]{2,1,0:T(8,128)(2,1)S(1)}, u32[]{:S(2)}) copy-start(bf16[8,128,256]{2,1,0:T(8,128)(2,1)S(1)} %all-to-all-done.1.parts_ref) | copy-start | bytes 1572868
  130.5 37.1 %all-to-all-start.3 = ((bf16[64,32,256]{2,1,0:T(8,128)(2,1)}), bf16[64,32,256]{2,1,0:T(8,128)(2,1)S(1)}, u32[]{:S(2)}, u32[]{:S(2)}) async-start(bf16[64,32,256]{2,1,0:T(8,128)(2,1)} %bitcast.8), calls=%async_computation.3 | async-start | bytes 2097152 | tf_op jit(solution)/shard_map/all_to_all | solution.py:216
  167.6 1.0 copy-start

commit v2 on v1

v2 whole, which is shorter than its diff:
```python
import math

import jax
import jax.numpy as jnp
from jax import lax
from jax.experimental import pallas as pl
from jax.experimental.pallas import tpu as pltpu
from jax.sharding import Mesh, PartitionSpec as P


BLOCK = 128
CHUNK = 512
SCORE_ROWS = 1024
GRAD_ROWS = 1024
DEAD = 1.0e30
F32 = jnp.float32
BF16 = jnp.bfloat16


def nt_dot(a, b):
    return lax.dot_general(a, b, (((1,), (1,)), ((), ())), preferred_element_type=F32)


def identity(size):
    rows = lax.broadcasted_iota(jnp.int32, (size, size), 0)
    cols = lax.broadcasted_iota(jnp.int32, (size, size), 1)
    return (rows == cols).astype(F32).astype(BF16)


def prepare_kernel(mask_ref, q_ref, dout_ref, q_out, dout_out, dead_ref):
    q_out[...] = q_ref[...]
    dout_out[...] = dout_ref[...]
    for j in range(dead_ref.shape[0]):
        dead = jnp.where(mask_ref[0, j] > 0, 0.0, DEAD)
        dead_ref[j : j + 1, :] = jnp.full((1, dead_ref.shape[1]), dead, F32)


def forward_kernel(
    dead_ref, kv_ref, q_ref, dout_ref, weights_ref, out_ref, stats_ref, peak_ref,
    scores_a, scores_b, wide,
):
    keys, width = kv_ref.shape[0], kv_ref.shape[1] // 2
    queries, heads = q_ref.shape[0], q_ref.shape[1] // width
    scale = 1.0 / math.sqrt(width)
    eye = identity(width)
    wide[width:, :] = jnp.ones((wide.shape[0] - width, keys), BF16)
    for start in range(0, keys, CHUNK):
        rows = slice(start, start + CHUNK)
        wide[:width, rows] = nt_dot(eye, kv_ref[rows, width:]).astype(BF16)
    scores = (scores_a, scores_b)
    tops = {}

    def score(h, start):
        query = q_ref[:, h * width : (h + 1) * width]
        block = nt_dot(kv_ref[start : start + SCORE_ROWS, :width], query) * scale
        scores[h % 2][start : start + SCORE_ROWS, :] = block
        for part in range(0, SCORE_ROWS, BLOCK):
            top = jnp.max(block[part : part + BLOCK].reshape(BLOCK // 8, 8, queries), axis=0)
            block_index = (start + part) // BLOCK
            top = top - dead_ref[block_index : block_index + 1, :]
            tops[h] = jnp.maximum(tops[h], top) if h in tops else top

    def weigh(h, j, peak):
        rows = slice(j * BLOCK, (j + 1) * BLOCK)
        block = jnp.exp(scores[h % 2][rows, :] - (peak + dead_ref[j : j + 1, :]))
        weights_ref[rows, h * queries : (h + 1) * queries] = block.astype(BF16)

    def combine(h, peak):
        lanes = slice(h * queries, (h + 1) * queries)
        acc = jnp.dot(wide[...], weights_ref[:, lanes], preferred_element_type=F32)
        total = acc[width : width + 1]
        out = acc[:width] / total
        out_ref[h] = out.astype(BF16)
        cotangent = nt_dot(eye, dout_ref[:, h * width : (h + 1) * width])
        stats_ref[h : h + 1, :] = peak + jnp.log(total)
        stats_ref[heads + h : heads + h + 1, :] = jnp.sum(cotangent * out, axis=0, keepdims=True)
        peak_ref[h : h + 1, :] = peak

    for start in range(0, keys, SCORE_ROWS):
        score(0, start)
    before = None
    for h in range(heads):
        peak = jnp.max(tops[h], axis=0, keepdims=True)
        for start in range(0, keys, SCORE_ROWS):
            if h + 1 < heads:
                score(h + 1, start)
            for j in range(start // BLOCK, (start + SCORE_ROWS) // BLOCK):
                weigh(h, j, peak)
        if before is not None:
            combine(h - 1, before)
        before = peak
    combine(heads - 1, before)


def row_mix(stats_ref, heads):
    panels = stats_ref.shape[0]
    top = stats_ref[0, :heads]
    for n in range(1, panels):
        top = jnp.maximum(top, stats_ref[n, :heads])
    total = jnp.zeros_like(top)
    delta = jnp.zeros_like(top)
    for n in range(panels):
        share = jnp.exp(stats_ref[n, :heads] - top)
        total = total + share
        delta = delta + share * stats_ref[n, heads:]
    return top + jnp.log(total), delta / total


def backward_kernel(
    stats_ref, peak_ref, own_ref, kv_ref, q_ref, dout_ref, weights_ref, out_ref,
    keep_ref, send_ref, dkv_ref, dscores, keys_t, mixed_q, mixed_dout, factors, blended,
):
    keys, width = kv_ref.shape[0], kv_ref.shape[1] // 2
    queries, heads = q_ref.shape[0], q_ref.shape[1] // width
    scale = 1.0 / math.sqrt(width)
    core = lax.axis_index("core")
    eye = identity(width)
    for start in range(0, keys, CHUNK):
        rows = slice(start, start + CHUNK)
        keys_t[:, rows] = nt_dot(eye, kv_ref[rows, :width]).astype(BF16)
    row_lse, row_delta = row_mix(stats_ref, heads)
    factor = jnp.exp(peak_ref[...] - row_lse)
    factors[:heads, :] = factor
    factors[heads : 2 * heads, :] = row_delta
    factors[2 * heads :, :] = jnp.exp(own_ref[:heads, :] - row_lse)
    columns = factor.T

    def mix(h):
        rows = slice(h * queries, (h + 1) * queries)
        cols = slice(h * width, (h + 1) * width)
        column = columns[:, h : h + 1]
        mixed_q[rows, :] = (q_ref[:, cols].astype(F32) * column).astype(BF16)
        mixed_dout[rows, :] = (dout_ref[:, cols].astype(F32) * column).astype(BF16)

    def differ(h, start):
        rows = slice(start, start + CHUNK)
        lanes = slice(h * queries, (h + 1) * queries)
        dprobs = nt_dot(kv_ref[rows, width:], dout_ref[:, h * width : (h + 1) * width])
        delta = factors[heads + h : heads + h + 1, :]
        dscores[rows, lanes] = (weights_ref[rows, lanes].astype(F32) * (dprobs - delta)).astype(BF16)

    def project(h):
        lanes = slice(h * queries, (h + 1) * queries)
        acc = jnp.dot(keys_t[...], dscores[:, lanes], preferred_element_type=F32)
        blended[h, :width, :] = (acc * (factors[h : h + 1, :] * scale)).astype(BF16)
        part = out_ref[h].astype(F32) * factors[2 * heads + h : 2 * heads + h + 1, :]
        blended[h, width:, :] = part.astype(BF16)

    for h in range(heads):
        for start in range(0, keys, CHUNK):
            differ(h, start)
        mix(h)
        if h:
            project(h - 1)
    project(heads - 1)

    def one_chunk(index, carry):
        rows = pl.ds(pl.multiple_of(index * GRAD_ROWS, GRAD_ROWS), GRAD_ROWS)
        key_part = jnp.dot(dscores[rows, :], mixed_q[...], preferred_element_type=F32)
        value_part = jnp.dot(weights_ref[rows, :], mixed_dout[...], preferred_element_type=F32)
        dkv_ref[rows, :width] = (key_part * scale).astype(BF16)
        dkv_ref[rows, width:] = value_part.astype(BF16)
        return carry

    lax.fori_loop(0, keys // GRAD_ROWS, one_chunk, 0)
    for index in range(heads // 2):
        keep_ref[index] = blended[2 * index + core]
        send_ref[index] = blended[2 * index + 1 - core]


def pair_kernel(keep_ref, got_ref, own_ref, one_ref, two_ref, three_ref):
    count = keep_ref.shape[0]
    place = lax.axis_index("y_hi")
    own_ref[...] = keep_ref[place].astype(F32) + got_ref[place].astype(F32)
    for step, target in enumerate((one_ref, two_ref, three_ref)):
        spot = lax.rem(place + step + 1, count)
        target[...] = (keep_ref[spot].astype(F32) + got_ref[spot].astype(F32)).astype(BF16)


def rows_kernel(own_ref, one_ref, two_ref, three_ref, query_grad_ref, attended_ref):
    width = query_grad_ref.shape[1]
    total = own_ref[...] + one_ref[...].astype(F32)
    total = total + two_ref[...].astype(F32) + three_ref[...].astype(F32)
    query_grad_ref[...] = total[:width].T
    attended_ref[...] = total[width:].T.astype(BF16)


def shards_kernel(parts_ref, key_grad_ref, value_grad_ref):
    width = key_grad_ref.shape[1]
    both = parts_ref[0].astype(F32)
    for n in range(1, parts_ref.shape[0]):
        both = both + parts_ref[n].astype(F32)
    key_grad_ref[...] = both[:, :width]
    value_grad_ref[...] = both[:, width:]


VMEM = pl.BlockSpec(memory_space=pltpu.VMEM)
SMEM = pl.BlockSpec(memory_space=pltpu.SMEM)


PB = ("y_lo", "x", "z")
KA = ("y_hi", "core")


def limit(mib):
    return pltpu.CompilerParams(vmem_limit_bytes=mib << 20)


def spread(block, axis):
    size = lax.axis_size(axis)
    copies = jnp.broadcast_to(block[None], (size,) + block.shape)
    return lax.all_to_all(copies, axis, 0, 0, tiled=True).reshape(-1, block.shape[1])


def per_device(queries, keys, values, dout, block_mask):
    rows, row_width = queries.shape
    shard, width = keys.shape
    heads = row_width // width
    pb, high = lax.axis_size(PB), lax.axis_size("y_hi")
    panel = shard * pb
    all_rows = heads * rows
    shape = jax.ShapeDtypeStruct

    kv = spread(jnp.concatenate([keys, values], axis=1), "z")
    kv = spread(kv, ("y_lo", "x"))

    q_near, dout_near, dead = pl.pallas_call(
        prepare_kernel,
        out_shape=(
            shape((rows, row_width), BF16),
            shape((rows, row_width), BF16),
            shape((panel // BLOCK, rows), F32),
        ),
        in_specs=[SMEM, VMEM, VMEM],
        out_specs=(VMEM,) * 3,
        compiler_params=limit(8),
        name="prepare",
    )(block_mask, queries, dout)

    weights, out_parts, stats, peak = pl.pallas_call(
        forward_kernel,
        out_shape=(
            shape((panel, all_rows), BF16),
            shape((heads, width, rows), BF16),
            shape((2 * heads, rows), F32),
            shape((heads, rows), F32),
        ),
        in_specs=[VMEM] * 4,
        out_specs=(VMEM,) * 4,
        scratch_shapes=[
            pltpu.VMEM((panel, rows), F32),
            pltpu.VMEM((panel, rows), F32),
            pltpu.VMEM((width + 16, panel), BF16),
        ],
        compiler_params=limit(20),
        name="forward",
    )(dead, kv, q_near, dout_near)

    all_stats = lax.all_gather(stats, KA)

    keep, send, dkv = pl.pallas_call(
        backward_kernel,
        out_shape=(
            shape((high, 2 * width, rows), BF16),
            shape((high, 2 * width, rows), BF16),
            shape((panel, 2 * width), BF16),
        ),
        in_specs=[VMEM] * 8,
        out_specs=(VMEM,) * 3,
        scratch_shapes=[
            pltpu.VMEM((panel, all_rows), BF16),
            pltpu.VMEM((width, panel), BF16),
            pltpu.VMEM((all_rows, width), BF16),
            pltpu.VMEM((all_rows, width), BF16),
            pltpu.VMEM((3 * heads, rows), F32),
            pltpu.VMEM((heads, 2 * width, rows), BF16),
        ],
        compiler_params=limit(30),
        name="backward",
    )(all_stats, peak, stats, kv, q_near, dout_near, weights, out_parts)

    dkv_own = lax.all_to_all(dkv.reshape(pb, shard, 2 * width), PB, 0, 0, tiled=True)
    got = lax.ppermute(send, "core", [(0, 1), (1, 0)])
    own, *moves = pl.pallas_call(
        pair_kernel,
        out_shape=(shape((2 * width, rows), F32),) + (shape((2 * width, rows), BF16),) * 3,
        in_specs=[VMEM, VMEM],
        out_specs=(VMEM,) * 4,
        compiler_params=limit(8),
        name="pair",
    )(keep, got)
    moved = [
        lax.ppermute(move, "y_hi", [(i, (i + step + 1) % high) for i in range(high)])
        for step, move in enumerate(moves)
    ]
    query_grad, attended = pl.pallas_call(
        rows_kernel,
        out_shape=(shape((rows, width), F32), shape((rows, width), BF16)),
        in_specs=[VMEM] * 4,
        out_specs=(VMEM,) * 2,
        compiler_params=limit(8),
        name="rows",
    )(own, *moved)
    key_grad, value_grad = pl.pallas_call(
        shards_kernel,
        out_shape=(shape((shard, width), F32), shape((shard, width), F32)),
        in_specs=[VMEM],
        out_specs=(VMEM,) * 2,
        compiler_params=limit(8),
        name="shards",
    )(dkv_own)
    return attended, query_grad, key_grad, value_grad


def solution(mesh):
    fine = Mesh(mesh.devices.reshape(2, 4, 8, 4, 2), PB + KA)
    split = P(KA + PB, None)
    in_specs = (P(PB, None), split, split, P(PB, None), P(PB, KA))
    out_specs = (P(PB, KA), P(PB, KA), split, split)

    return jax.shard_map(
        per_device, mesh=fine, in_specs=in_specs, out_specs=out_specs, check_vma=False
    )
```

time: 171 us -> 108 us (0.63)
  the two profiles are of different devices: /device:TPU:9 before, /device:TPU:1 now
where the time goes in v2:
time: 108 us
  blocking collectives  38.8 us (36%)
  starting transfers between devices  25.1 us (23%)
  waiting for transfers between devices  21 us (19%)
  Pallas kernels  17.7 us (16%)
  local copies, waits for them, and re-layouts  3.81 us (4%)
    all_gather x1, blocking collectives, per_device(): all_stats = lax.all_gather(stats, KA)  20.4 us
    all_to_all x1, blocking collectives, spread(): lax.all_to_all(copies, axis, 0, 0, tiled=True).reshape(-1, block.shape[1])  18.4 us
    ppermute x3, starting transfers between devices, per_device(): lax.ppermute(move, 'y_hi', [(i, (i + step + 1) % high) for i in range(hig...  12.6 us
    pallas_call x1, Pallas kernels, per_device(): pl.pallas_call(backward_kernel, out_shape=(shape((high, 2 * width, rows),...  9.8 us
    ppermute x3, waiting for transfers between devices, per_device(): lax.ppermute(move, 'y_hi', [(i, (i + step + 1) % high) for i in range(hig...  9.09 us
    all_to_all x1, waiting for transfers between devices, spread(): lax.all_to_all(copies, axis, 0, 0, tiled=True).reshape(-1, block.shape[1])  7.89 us
    pallas_call x1, Pallas kernels, per_device(): pl.pallas_call(forward_kernel, out_shape=(shape((panel, all_rows), BF16),...  5.57 us
    all_to_all x1, starting transfers between devices, per_device(): lax.all_to_all(dkv.reshape(pb, shard, 2 * width), PB, 0, 0, tiled=True)  5.07 us
  transfers between devices with their start and end apart: 6, of which 6 were waited for; matrix products, arithmetic and copies ran while one was open for 0% of the time, Pallas kernels for 1%

profile of v2, /device:TPU:1, one launch (start us, length us, event | category | flops | bytes accessed | tf_op | source)
XLA Modules:
  0.0 107.8 jit_solution(6274351035112434807)
XLA Ops:
  0.6 0.7 pad_maximum_fusion
  1.4 18.4 %all_to_all.15 = bf16[8,32,256]{2,1,0:T(8,128)(2,1)S(1)} all-to-all(bf16[8,32,256]{2,1,0:T(8,128)(2,1)S(1)} %broadcast_in_dim.6), channel_id=1, replica_groups=mesh['y_lo'=2,'x'=4,'z'=8,'y_hi'=4,'core'=2] {'z'}, dimensions={0} | all-to-all | bytes 262144 | tf_op jit(solution)/shard_map/all_to_all | solution.py:212
  19.8 1.0 broadcast_in_dim.15
  20.8 5.0 %all-to-all-start.1 = ((bf16[8,256,256]{2,1,0:T(8,128)(2,1)}), bf16[8,256,256]{2,1,0:T(8,128)(2,1)S(1)}, u32[]{:S(2)}, u32[]{:S(2)}) async-start(bf16[8,256,256]{2,1,0:T(8,128)(2,1)} %broadcast_in_dim.15), calls=%async_computation.1 | async-start | bytes 2097152 | tf_op jit(solution)/shard_map/all_to_all | solution.py:212
  25.8 1.0 copy-done
  26.9 1.0 copy-done.1
  27.9 0.7 copy-done.2
  28.6 0.6 prepare.1
  29.2 7.9 %all-to-all-done.1 = bf16[8,256,256]{2,1,0:T(8,128)(2,1)S(1)} async-done(((bf16[8,256,256]{2,1,0:T(8,128)(2,1)}), bf16[8,256,256]{2,1,0:T(8,128)(2,1)S(1)}, u32[]{:S(2)}, u32[]{:S(2)}) %all-to-all-start.1) | async-done | bytes 1048608 | tf_op jit(solution)/shard_map/all_to_all | solution.py:212
  37.1 5.6 %forward.1 = (bf16[2048,2048]{1,0:T(8,128)(2,1)S(1)}, bf16[8,128,256]{2,1,0:T(8,128)(2,1)S(1)}, f32[16,256]{1,0:T(8,128)S(1)}, f32[8,256]{1,0:T(8,128)S(1)}) custom-call(f32[16,256]{1,0:T(8,128)S(1)} %get-tuple-element.22.dead_ref, bf16[2048,256]{1,0:T(8,128)(2,1)S(1)} %bitcast.4, bf16[256,1024]{1,0:T(8,128)(2,1)S(1)} %get-tuple-element.23.q_ref, ...), custom_call_target="tpu_custom_call" | custom-call | tf_op jit(solution)/shard_map/forward/pallas_call | solution.py:240
  42.7 20.4 %all-gather = f32[128,256]{1,0:T(8,128)S(1)} all-gather(f32[16,256]{1,0:T(8,128)S(1)} %get-tuple-element.25.own_ref), channel_id=2, replica_groups=mesh['y_lo'=2,'x'=4,'z'=8,'y_hi'=4,'core'=2] {'y_hi','core'}, dimensions={0}, use_global_device_ids=true | all-gather | bytes 147456 | tf_op jit(solution)/shard_map/all_gather | solution.py:259
  63.1 9.8 %backward.1 = (bf16[4,256,256]{2,1,0:T(8,128)(2,1)S(1)}, bf16[4,256,256]{2,1,0:T(8,128)(2,1)S(1)}, bf16[2048,256]{1,0:T(8,128)(2,1)}) custom-call(f32[8,16,256]{2,1,0:T(8,128)S(1)} %bitcast.6, f32[8,256]{1,0:T(8,128)S(1)} %get-tuple-element.26.peak_ref, f32[16,256]{1,0:T(8,128)S(1)} %get-tuple-element.25.own_ref, bf16[2048,256]{1,0:T(8,128)(2,1)S(1)} %bitcast.5, ...), custom_call_target="tpu_custom_call" | custom-call | tf_op jit(solution)/shard_map/backward/pallas_call | solution.py:261
  72.9 5.1 %all-to-all-start.2 = ((bf16[64,32,256]{2,1,0:T(8,128)(2,1)}), bf16[64,32,256]{2,1,0:T(8,128)(2,1)S(1)}, u32[]{:S(2)}, u32[]{:S(2)}) async-start(bf16[64,32,256]{2,1,0:T(8,128)(2,1)} %bitcast.3), calls=%async_computation.2 | async-start | bytes 2097152 | tf_op jit(solution)/shard_map/all_to_all | solution.py:282
  78.0 2.3 %collective-permute-start = (bf16[4,256,256]{2,1,0:T(8,128)(2,1)S(1)}, bf16[4,256,256]{2,1,0:T(8,128)(2,1)S(1)}, u32[]{:S(2)}, u32[]{:S(2)}) collective-permute-start(bf16[4,256,256]{2,1,0:T(8,128)(2,1)S(1)} %get-tuple-element.30), channel_id=1, source_target_pairs={{0,1},{1,0},{2,3},{3,2},{4,5},{5,4},{6,7},{7,6},{8,9},{9,8},{10,11... | collective-permute-start | bytes 1572872 | tf_op jit(solution)/shard_map/ppermute | solution.py:283
  80.3 1.5 %collective-permute-done.got_ref = bf16[4,256,256]{2,1,0:T(8,128)(2,1)S(1)} collective-permute-done((bf16[4,256,256]{2,1,0:T(8,128)(2,1)S(1)}, bf16[4,256,256]{2,1,0:T(8,128)(2,1)S(1)}, u32[]{:S(2)}, u32[]{:S(2)}) %collective-permute-start) | collective-permute-done | bytes 524320 | tf_op jit(solution)/shard_map/ppermute | solution.py:283
  82.0 2.9 %collective-permute-start.1 = (bf16[256,256]{1,0:T(8,128)(2,1)S(1)}, bf16[256,256]{1,0:T(8,128)(2,1)S(1)}, u32[]{:S(2)}, u32[]{:S(2)}) collective-permute-start(bf16[256,256]{1,0:T(8,128)(2,1)S(1)} %get-tuple-element.32), channel_id=1, source_target_pairs={{0,2},{2,4},{4,6},{6,0},{1,3},{3,5},{5,7},{7,1},{8,10},{10,12},{12... | collective-permute-start | bytes 393224 | tf_op jit(solution)/shard_map/ppermute | solution.py:293
  84.9 4.8 %collective-permute-start.2 = (bf16[256,256]{1,0:T(8,128)(2,1)S(1)}, bf16[256,256]{1,0:T(8,128)(2,1)S(1)}, u32[]{:S(2)}, u32[]{:S(2)}) collective-permute-start(bf16[256,256]{1,0:T(8,128)(2,1)S(1)} %get-tuple-element.33), channel_id=1, source_target_pairs={{0,4},{2,6},{4,0},{6,2},{1,5},{3,7},{5,1},{7,3},{8,12},{10,14},{12... | collective-permute-start | bytes 393224 | tf_op jit(solution)/shard_map/ppermute | solution.py:293
  89.6 5.0 %collective-permute-start.3 = (bf16[256,256]{1,0:T(8,128)(2,1)S(1)}, bf16[256,256]{1,0:T(8,128)(2,1)S(1)}, u32[]{:S(2)}, u32[]{:S(2)}) collective-permute-start(bf16[256,256]{1,0:T(8,128)(2,1)S(1)} %get-tuple-element.34), channel_id=1, source_target_pairs={{0,6},{2,0},{4,2},{6,4},{1,7},{3,1},{5,3},{7,5},{8,14},{10,8},{12,... | collective-permute-start | bytes 393224 | tf_op jit(solution)/shard_map/ppermute | solution.py:293
  94.6 2.5 %collective-permute-done.1.one_ref = bf16[256,256]{1,0:T(8,128)(2,1)S(1)} collective-permute-done((bf16[256,256]{1,0:T(8,128)(2,1)S(1)}, bf16[256,256]{1,0:T(8,128)(2,1)S(1)}, u32[]{:S(2)}, u32[]{:S(2)}) %collective-permute-start.1) | collective-permute-done | bytes 131104 | tf_op jit(solution)/shard_map/ppermute | solution.py:293
  97.1 6.1 %collective-permute-done.2.two_ref = bf16[256,256]{1,0:T(8,128)(2,1)S(1)} collective-permute-done((bf16[256,256]{1,0:T(8,128)(2,1)S(1)}, bf16[256,256]{1,0:T(8,128)(2,1)S(1)}, u32[]{:S(2)}, u32[]{:S(2)}) %collective-permute-start.2) | collective-permute-done | bytes 131104 | tf_op jit(solution)/shard_map/ppermute | solution.py:293
  103.2 0.5 collective-permute-done.3.three_ref
  103.7 0.8 rows.1
  104.5 2.5 %all-to-all-done.2.parts_ref = bf16[64,32,256]{2,1,0:T(8,128)(2,1)S(1)} async-done(((bf16[64,32,256]{2,1,0:T(8,128)(2,1)}), bf16[64,32,256]{2,1,0:T(8,128)(2,1)S(1)}, u32[]{:S(2)}, u32[]{:S(2)}) %all-to-all-start.2) | async-done | bytes 1048608 | tf_op jit(solution)/shard_map/all_to_all | solution.py:282
  107.0 0.8 shards.1
  (5 shorter events, 0.1 us)
Async XLA Ops:
  20.8 16.3 %all-to-all-start.1 = ((bf16[8,256,256]{2,1,0:T(8,128)(2,1)}), bf16[8,256,256]{2,1,0:T(8,128)(2,1)S(1)}, u32[]{:S(2)}, u32[]{:S(2)}) async-start(bf16[8,256,256]{2,1,0:T(8,128)(2,1)} %broadcast_in_dim.15), calls=%async_computation.1 | async-start | bytes 2097152 | tf_op jit(solution)/shard_map/all_to_all | solution.py:212
  25.8 1.0 copy-start
  26.9 1.0 copy-start.1
  27.9 0.7 copy-start.2
  72.9 34.1 %all-to-all-start.2 = ((bf16[64,32,256]{2,1,0:T(8,128)(2,1)}), bf16[64,32,256]{2,1,0:T(8,128)(2,1)S(1)}, u32[]{:S(2)}, u32[]{:S(2)}) async-start(bf16[64,32,256]{2,1,0:T(8,128)(2,1)} %bitcast.3), calls=%async_computation.2 | async-start | bytes 2097152 | tf_op jit(solution)/shard_map/all_to_all | solution.py:282
  78.0 3.9 %collective-permute-start = (bf16[4,256,256]{2,1,0:T(8,128)(2,1)S(1)}, bf16[4,256,256]{2,1,0:T(8,128)(2,1)S(1)}, u32[]{:S(2)}, u32[]{:S(2)}) collective-permute-start(bf16[4,256,256]{2,1,0:T(8,128)(2,1)S(1)} %get-tuple-element.30), channel_id=1, source_target_pairs={{0,1},{1,0},{2,3},{3,2},{4,5},{5,4},{6,7},{7,6},{8,9},{9,8},{10,11... | collective-permute-start | bytes 1572872 | tf_op jit(solution)/shard_map/ppermute | solution.py:283
  82.0 15.1 %collective-permute-start.1 = (bf16[256,256]{1,0:T(8,128)(2,1)S(1)}, bf16[256,256]{1,0:T(8,128)(2,1)S(1)}, u32[]{:S(2)}, u32[]{:S(2)}) collective-permute-start(bf16[256,256]{1,0:T(8,128)(2,1)S(1)} %get-tuple-element.32), channel_id=1, source_target_pairs={{0,2},{2,4},{4,6},{6,0},{1,3},{3,5},{5,7},{7,1},{8,10},{10,12},{12... | collective-permute-start | bytes 393224 | tf_op jit(solution)/shard_map/ppermute | solution.py:293
  84.9 18.4 %collective-permute-start.2 = (bf16[256,256]{1,0:T(8,128)(2,1)S(1)}, bf16[256,256]{1,0:T(8,128)(2,1)S(1)}, u32[]{:S(2)}, u32[]{:S(2)}) collective-permute-start(bf16[256,256]{1,0:T(8,128)(2,1)S(1)} %get-tuple-element.33), channel_id=1, source_target_pairs={{0,4},{2,6},{4,0},{6,2},{1,5},{3,7},{5,1},{7,3},{8,12},{10,14},{12... | collective-permute-start | bytes 393224 | tf_op jit(solution)/shard_map/ppermute | solution.py:293
  89.6 14.1 %collective-permute-start.3 = (bf16[256,256]{1,0:T(8,128)(2,1)S(1)}, bf16[256,256]{1,0:T(8,128)(2,1)S(1)}, u32[]{:S(2)}, u32[]{:S(2)}) collective-permute-start(bf16[256,256]{1,0:T(8,128)(2,1)S(1)} %get-tuple-element.34), channel_id=1, source_target_pairs={{0,6},{2,0},{4,2},{6,4},{1,7},{3,1},{5,3},{7,5},{8,14},{10,8},{12,... | collective-permute-start | bytes 393224 | tf_op jit(solution)/shard_map/ppermute | solution.py:293

commit v3 on v2

--- a/solution.py
+++ b/solution.py
@@ -27,26 +27,29 @@
     return (rows == cols).astype(F32).astype(BF16)
 
 
-def prepare_kernel(mask_ref, q_ref, dout_ref, q_out, dout_out, dead_ref):
-    q_out[...] = q_ref[...]
-    dout_out[...] = dout_ref[...]
-    for j in range(dead_ref.shape[0]):
-        dead = jnp.where(mask_ref[0, j] > 0, 0.0, DEAD)
-        dead_ref[j : j + 1, :] = jnp.full((1, dead_ref.shape[1]), dead, F32)
-
-
 def forward_kernel(
-    dead_ref, kv_ref, q_ref, dout_ref, weights_ref, out_ref, stats_ref, peak_ref,
-    scores_a, scores_b, wide,
+    mask_hbm, kv_ref, q_hbm, dout_hbm, weights_ref, out_ref, copies_ref, peak_ref, q_ref, dout_ref,
+    stats_ref, scores_a, scores_b, wide, mask_ref, sems,
 ):
     keys, width = kv_ref.shape[0], kv_ref.shape[1] // 2
     queries, heads = q_ref.shape[0], q_ref.shape[1] // width
     scale = 1.0 / math.sqrt(width)
+    loads = [
+        pltpu.make_async_copy(mask_hbm, mask_ref, sems.at[0]),
+        pltpu.make_async_copy(q_hbm.at[:, :width], q_ref.at[:, :width], sems.at[1]),
+        pltpu.make_async_copy(q_hbm.at[:, width:], q_ref.at[:, width:], sems.at[2]),
+        pltpu.make_async_copy(dout_hbm, dout_ref, sems.at[3]),
+    ]
+    for load in loads:
+        load.start()
     eye = identity(width)
     wide[width:, :] = jnp.ones((wide.shape[0] - width, keys), BF16)
     for start in range(0, keys, CHUNK):
         rows = slice(start, start + CHUNK)
         wide[:width, rows] = nt_dot(eye, kv_ref[rows, width:]).astype(BF16)
+    loads[0].wait()
+    loads[1].wait()
+    dead = [jnp.where(mask_ref[0, j] > 0, 0.0, DEAD) for j in range(keys // BLOCK)]
     scores = (scores_a, scores_b)
     tops = {}
 
@@ -56,13 +59,12 @@
         scores[h % 2][start : start + SCORE_ROWS, :] = block
         for part in range(0, SCORE_ROWS, BLOCK):
             top = jnp.max(block[part : part + BLOCK].reshape(BLOCK // 8, 8, queries), axis=0)
-            block_index = (start + part) // BLOCK
-            top = top - dead_ref[block_index : block_index + 1, :]
+            top = top - dead[(start + part) // BLOCK]
             tops[h] = jnp.maximum(tops[h], top) if h in tops else top
 
     def weigh(h, j, peak):
         rows = slice(j * BLOCK, (j + 1) * BLOCK)
-        block = jnp.exp(scores[h % 2][rows, :] - (peak + dead_ref[j : j + 1, :]))
+        block = jnp.exp(scores[h % 2][rows, :] - (peak + dead[j]))
         weights_ref[rows, h * queries : (h + 1) * queries] = block.astype(BF16)
 
     def combine(h, peak):
@@ -78,6 +80,7 @@
 
     for start in range(0, keys, SCORE_ROWS):
         score(0, start)
+    loads[2].wait()
     before = None
     for h in range(heads):
         peak = jnp.max(tops[h], axis=0, keepdims=True)
@@ -87,9 +90,13 @@
             for j in range(start // BLOCK, (start + SCORE_ROWS) // BLOCK):
                 weigh(h, j, peak)
         if before is not None:
+            if h == 1:
+                loads[3].wait()
             combine(h - 1, before)
         before = peak
     combine(heads - 1, before)
+    for n in range(copies_ref.shape[0]):
+        copies_ref[n] = stats_ref[...]
 
 
 def row_mix(stats_ref, heads):
@@ -122,7 +129,7 @@
     factor = jnp.exp(peak_ref[...] - row_lse)
     factors[:heads, :] = factor
     factors[heads : 2 * heads, :] = row_delta
-    factors[2 * heads :, :] = jnp.exp(own_ref[:heads, :] - row_lse)
+    factors[2 * heads :, :] = jnp.exp(own_ref[0, :heads] - row_lse)
     columns = factor.T
 
     def mix(h):
@@ -195,7 +202,7 @@
 
 
 VMEM = pl.BlockSpec(memory_space=pltpu.VMEM)
-SMEM = pl.BlockSpec(memory_space=pltpu.SMEM)
+FAR = pl.BlockSpec(memory_space=pltpu.HBM)
 
 
 PB = ("y_lo", "x", "z")
@@ -224,39 +231,36 @@
     kv = spread(jnp.concatenate([keys, values], axis=1), "z")
     kv = spread(kv, ("y_lo", "x"))
 
-    q_near, dout_near, dead = pl.pallas_call(
-        prepare_kernel,
-        out_shape=(
-            shape((rows, row_width), BF16),
-            shape((rows, row_width), BF16),
-            shape((panel // BLOCK, rows), F32),
-        ),
-        in_specs=[SMEM, VMEM, VMEM],
-        out_specs=(VMEM,) * 3,
-        compiler_params=limit(8),
-        name="prepare",
-    )(block_mask, queries, dout)
-
-    weights, out_parts, stats, peak = pl.pallas_call(
+    weights, out_parts, stats, peak, q_near, dout_near = pl.pallas_call(
         forward_kernel,
         out_shape=(
             shape((panel, all_rows), BF16),
             shape((heads, width, rows), BF16),
-            shape((2 * heads, rows), F32),
+            shape((lax.axis_size(KA), 2 * heads, rows), F32),
             shape((heads, rows), F32),
+            shape((rows, row_width), BF16),
+            shape((rows, row_width), BF16),
         ),
-        in_specs=[VMEM] * 4,
-        out_specs=(VMEM,) * 4,
+        in_specs=[FAR, VMEM, FAR, FAR],
+        out_specs=(VMEM,) * 6,
         scratch_shapes=[
+            pltpu.VMEM((2 * heads, rows), F32),
             pltpu.VMEM((panel, rows), F32),
             pltpu.VMEM((panel, rows), F32),
             pltpu.VMEM((width + 16, panel), BF16),
+            pltpu.SMEM(block_mask.shape, jnp.int32),
+            pltpu.SemaphoreType.DMA((4,)),
         ],
         compiler_params=limit(20),
         name="forward",
-    )(dead, kv, q_near, dout_near)
-
-    all_stats = lax.all_gather(stats, KA)
+    )(
+        *(
+            x if x is kv else pltpu.with_memory_space_constraint(x, pltpu.HBM)
+            for x in (block_mask, kv, queries, dout)
+        )
+    )
+
+    all_stats = lax.all_to_all(stats, KA, 0, 0, tiled=True)
 
     keep, send, dkv = pl.pallas_call(
         backward_kernel,

time: 108 us -> 107 us (level)
  the two profiles are of different devices: /device:TPU:1 before, /device:TPU:9 now
where the time goes in v3:
time: 107 us
  blocking collectives  52.2 us (49%)
  starting transfers between devices  19 us (18%)
  Pallas kernels  18.8 us (18%)
  waiting for transfers between devices  15.3 us (14%)
    all_to_all x2, blocking collectives, spread(): lax.all_to_all(copies, axis, 0, 0, tiled=True).reshape(-1, block.shape[1])  34.6 us
    all_to_all x1, blocking collectives, per_device(): all_stats = lax.all_to_all(stats, KA, 0, 0, tiled=True)  17.6 us
    ppermute x3, starting transfers between devices, per_device(): lax.ppermute(move, 'y_hi', [(i, (i + step + 1) % high) for i in range(hig...  10.1 us
    pallas_call x1, Pallas kernels, per_device(): pl.pallas_call(backward_kernel, out_shape=(shape((high, 2 * width, rows),...  10.1 us
    ppermute x3, waiting for transfers between devices, per_device(): lax.ppermute(move, 'y_hi', [(i, (i + step + 1) % high) for i in range(hig...  9.55 us
    pallas_call x1, Pallas kernels, per_device(): pl.pallas_call(forward_kernel, out_shape=(shape((panel, all_rows), BF16),...  7.03 us
    all_to_all x1, starting transfers between devices, per_device(): lax.all_to_all(dkv.reshape(pb, shard, 2 * width), PB, 0, 0, tiled=True)  5.42 us
    all_to_all x1, waiting for transfers between devices, per_device(): lax.all_to_all(dkv.reshape(pb, shard, 2 * width), PB, 0, 0, tiled=True)  4.27 us
  transfers between devices with their start and end apart: 5, of which 4 were waited for; matrix products, arithmetic and copies ran while one was open for 0% of the time, Pallas kernels for 1%

profile of v3, /device:TPU:9, one launch (start us, length us, event | category | flops | bytes accessed | tf_op | source)
XLA Modules:
  0.0 106.9 jit_solution(14439821983763840117)
XLA Ops:
  0.6 0.7 pad_maximum_fusion
  1.4 17.6 %all_to_all.20 = bf16[8,32,256]{2,1,0:T(8,128)(2,1)S(1)} all-to-all(bf16[8,32,256]{2,1,0:T(8,128)(2,1)S(1)} %broadcast_in_dim.6), channel_id=1, replica_groups=mesh['y_lo'=2,'x'=4,'z'=8,'y_hi'=4,'core'=2] {'z'}, dimensions={0} | all-to-all | bytes 262144 | tf_op jit(solution)/shard_map/all_to_all | solution.py:219
  18.9 0.1 broadcast_in_dim.15
  19.0 17.0 %all_to_all.21 = bf16[8,256,256]{2,1,0:T(8,128)(2,1)S(1)} all-to-all(bf16[8,256,256]{2,1,0:T(8,128)(2,1)S(1)} %broadcast_in_dim.15), channel_id=1, replica_groups=mesh['y_lo'=2,'x'=4,'z'=8,'y_hi'=4,'core'=2] {'y_lo','x'}, dimensions={0} | all-to-all | bytes 2097152 | tf_op jit(solution)/shard_map/all_to_all | solution.py:219
  36.1 7.0 %forward.1 = (bf16[2048,2048]{1,0:T(8,128)(2,1)S(1)}, bf16[8,128,256]{2,1,0:T(8,128)(2,1)S(1)}, f32[8,16,256]{2,1,0:T(8,128)S(1)}, f32[8,256]{1,0:T(8,128)S(1)},...) custom-call(s32[2,16]{1,0:T(2,128)} %mask_hbm.1, bf16[2048,256]{1,0:T(8,128)(2,1)S(1)} %bitcast.3, ...), custom_call_target="tpu_custom_call" | custom-call | tf_op jit(solution)/shard_map/forward/pallas_call | solution.py:234
  43.1 17.6 %all_to_all.22.stats_ref = f32[8,16,256]{2,1,0:T(8,128)S(1)} all-to-all(f32[8,16,256]{2,1,0:T(8,128)S(1)} %get-tuple-element.21.own_ref), channel_id=1, replica_groups=mesh['y_lo'=2,'x'=4,'z'=8,'y_hi'=4,'core'=2] {'y_hi','core'}, dimensions={0} | all-to-all | bytes 262144 | tf_op jit(solution)/shard_map/all_to_all | solution.py:263
  60.7 10.1 %backward.1 = (bf16[4,256,256]{2,1,0:T(8,128)(2,1)S(1)}, bf16[4,256,256]{2,1,0:T(8,128)(2,1)S(1)}, bf16[2048,256]{1,0:T(8,128)(2,1)}) custom-call(f32[8,16,256]{2,1,0:T(8,128)S(1)} %all_to_all.22.stats_ref, f32[8,256]{1,0:T(8,128)S(1)} %get-tuple-element.22.peak_ref, f32[8,16,256]{2,1,0:T(8,128)S(1)} %get-tuple-element.21.own_ref, ...), custom_call_target="tpu_custom_call" | custom-call | tf_op jit(solution)/shard_map/backward/pallas_call | solution.py:265
  70.7 5.4 %all-to-all-start.3 = ((bf16[64,32,256]{2,1,0:T(8,128)(2,1)}), bf16[64,32,256]{2,1,0:T(8,128)(2,1)S(1)}, u32[]{:S(2)}, u32[]{:S(2)}) async-start(bf16[64,32,256]{2,1,0:T(8,128)(2,1)} %bitcast.2), calls=%async_computation.3 | async-start | bytes 2097152 | tf_op jit(solution)/shard_map/all_to_all | solution.py:286
  76.2 3.5 %collective-permute-start = (bf16[4,256,256]{2,1,0:T(8,128)(2,1)S(1)}, bf16[4,256,256]{2,1,0:T(8,128)(2,1)S(1)}, u32[]{:S(2)}, u32[]{:S(2)}) collective-permute-start(bf16[4,256,256]{2,1,0:T(8,128)(2,1)S(1)} %get-tuple-element.28), channel_id=1, source_target_pairs={{0,1},{1,0},{2,3},{3,2},{4,5},{5,4},{6,7},{7,6},{8,9},{9,8},{10,11... | collective-permute-start | bytes 1572872 | tf_op jit(solution)/shard_map/ppermute | solution.py:287
  79.7 1.5 %collective-permute-done.got_ref = bf16[4,256,256]{2,1,0:T(8,128)(2,1)S(1)} collective-permute-done((bf16[4,256,256]{2,1,0:T(8,128)(2,1)S(1)}, bf16[4,256,256]{2,1,0:T(8,128)(2,1)S(1)}, u32[]{:S(2)}, u32[]{:S(2)}) %collective-permute-start) | collective-permute-done | bytes 524320 | tf_op jit(solution)/shard_map/ppermute | solution.py:287
  81.2 0.1 pair.1
  81.3 2.2 %collective-permute-start.1 = (bf16[256,256]{1,0:T(8,128)(2,1)S(1)}, bf16[256,256]{1,0:T(8,128)(2,1)S(1)}, u32[]{:S(2)}, u32[]{:S(2)}) collective-permute-start(bf16[256,256]{1,0:T(8,128)(2,1)S(1)} %get-tuple-element.30), channel_id=1, source_target_pairs={{0,2},{2,4},{4,6},{6,0},{1,3},{3,5},{5,7},{7,1},{8,10},{10,12},{12... | collective-permute-start | bytes 393224 | tf_op jit(solution)/shard_map/ppermute | solution.py:297
  83.5 4.3 %collective-permute-start.2 = (bf16[256,256]{1,0:T(8,128)(2,1)S(1)}, bf16[256,256]{1,0:T(8,128)(2,1)S(1)}, u32[]{:S(2)}, u32[]{:S(2)}) collective-permute-start(bf16[256,256]{1,0:T(8,128)(2,1)S(1)} %get-tuple-element.31), channel_id=1, source_target_pairs={{0,4},{2,6},{4,0},{6,2},{1,5},{3,7},{5,1},{7,3},{8,12},{10,14},{12... | collective-permute-start | bytes 393224 | tf_op jit(solution)/shard_map/ppermute | solution.py:297
  87.8 3.6 %collective-permute-start.3 = (bf16[256,256]{1,0:T(8,128)(2,1)S(1)}, bf16[256,256]{1,0:T(8,128)(2,1)S(1)}, u32[]{:S(2)}, u32[]{:S(2)}) collective-permute-start(bf16[256,256]{1,0:T(8,128)(2,1)S(1)} %get-tuple-element.32), channel_id=1, source_target_pairs={{0,6},{2,0},{4,2},{6,4},{1,7},{3,1},{5,3},{7,5},{8,14},{10,8},{12,... | collective-permute-start | bytes 393224 | tf_op jit(solution)/shard_map/ppermute | solution.py:297
  91.4 0.0 collective-permute-done.1.one_ref
  91.4 4.5 %collective-permute-done.2.two_ref = bf16[256,256]{1,0:T(8,128)(2,1)S(1)} collective-permute-done((bf16[256,256]{1,0:T(8,128)(2,1)S(1)}, bf16[256,256]{1,0:T(8,128)(2,1)S(1)}, u32[]{:S(2)}, u32[]{:S(2)}) %collective-permute-start.2) | collective-permute-done | bytes 131104 | tf_op jit(solution)/shard_map/ppermute | solution.py:297
  96.0 5.0 %collective-permute-done.3.three_ref = bf16[256,256]{1,0:T(8,128)(2,1)S(1)} collective-permute-done((bf16[256,256]{1,0:T(8,128)(2,1)S(1)}, bf16[256,256]{1,0:T(8,128)(2,1)S(1)}, u32[]{:S(2)}, u32[]{:S(2)}) %collective-permute-start.3) | collective-permute-done | bytes 131104 | tf_op jit(solution)/shard_map/ppermute | solution.py:297
  101.0 0.8 rows.1
  101.8 4.3 %all-to-all-done.3.parts_ref = bf16[64,32,256]{2,1,0:T(8,128)(2,1)S(1)} async-done(((bf16[64,32,256]{2,1,0:T(8,128)(2,1)}), bf16[64,32,256]{2,1,0:T(8,128)(2,1)S(1)}, u32[]{:S(2)}, u32[]{:S(2)}) %all-to-all-start.3) | async-done | bytes 1048608 | tf_op jit(solution)/shard_map/all_to_all | solution.py:286
  106.1 0.8 shards.1
  (1 shorter events, 0.0 us)
Async XLA Ops:
  70.7 35.3 %all-to-all-start.3 = ((bf16[64,32,256]{2,1,0:T(8,128)(2,1)}), bf16[64,32,256]{2,1,0:T(8,128)(2,1)S(1)}, u32[]{:S(2)}, u32[]{:S(2)}) async-start(bf16[64,32,256]{2,1,0:T(8,128)(2,1)} %bitcast.2), calls=%async_computation.3 | async-start | bytes 2097152 | tf_op jit(solution)/shard_map/all_to_all | solution.py:286
  76.2 5.0 %collective-permute-start = (bf16[4,256,256]{2,1,0:T(8,128)(2,1)S(1)}, bf16[4,256,256]{2,1,0:T(8,128)(2,1)S(1)}, u32[]{:S(2)}, u32[]{:S(2)}) collective-permute-start(bf16[4,256,256]{2,1,0:T(8,128)(2,1)S(1)} %get-tuple-element.28), channel_id=1, source_target_pairs={{0,1},{1,0},{2,3},{3,2},{4,5},{5,4},{6,7},{7,6},{8,9},{9,8},{10,11... | collective-permute-start | bytes 1572872 | tf_op jit(solution)/shard_map/ppermute | solution.py:287
  81.3 10.1 %collective-permute-start.1 = (bf16[256,256]{1,0:T(8,128)(2,1)S(1)}, bf16[256,256]{1,0:T(8,128)(2,1)S(1)}, u32[]{:S(2)}, u32[]{:S(2)}) collective-permute-start(bf16[256,256]{1,0:T(8,128)(2,1)S(1)} %get-tuple-element.30), channel_id=1, source_target_pairs={{0,2},{2,4},{4,6},{6,0},{1,3},{3,5},{5,7},{7,1},{8,10},{10,12},{12... | collective-permute-start | bytes 393224 | tf_op jit(solution)/shard_map/ppermute | solution.py:297
  83.5 12.5 %collective-permute-start.2 = (bf16[256,256]{1,0:T(8,128)(2,1)S(1)}, bf16[256,256]{1,0:T(8,128)(2,1)S(1)}, u32[]{:S(2)}, u32[]{:S(2)}) collective-permute-start(bf16[256,256]{1,0:T(8,128)(2,1)S(1)} %get-tuple-element.31), channel_id=1, source_target_pairs={{0,4},{2,6},{4,0},{6,2},{1,5},{3,7},{5,1},{7,3},{8,12},{10,14},{12... | collective-permute-start | bytes 393224 | tf_op jit(solution)/shard_map/ppermute | solution.py:297
  87.8 13.2 %collective-permute-start.3 = (bf16[256,256]{1,0:T(8,128)(2,1)S(1)}, bf16[256,256]{1,0:T(8,128)(2,1)S(1)}, u32[]{:S(2)}, u32[]{:S(2)}) collective-permute-start(bf16[256,256]{1,0:T(8,128)(2,1)S(1)} %get-tuple-element.32), channel_id=1, source_target_pairs={{0,6},{2,0},{4,2},{6,4},{1,7},{3,1},{5,3},{7,5},{8,14},{10,8},{12,... | collective-permute-start | bytes 393224 | tf_op jit(solution)/shard_map/ppermute | solution.py:297
